TPU v7x, 256 devices: a whole 4x4x8 slice. The times are simulated.
256 devices in a mesh: cell: 64 (over x, z, core), blk: 4 (over y).
Axes of the slice: x: 4, y: 4, z: 8, core: 2. Of those that a mesh axis runs over, the one named last changes fastest.
Arguments:
- velocity_modes: bfloat16 [8, 3, 2, 256, 256, 128], P('blk', None, None, None, 'cell'), may hold values from -6 to 6
- block_list: int32 [2, 2], replicated, may hold values from 0 to 2, as said below
- counts: int32 [2], replicated, may hold values from 1 to 64, as said below
Outputs:
- transfer: float32 [192, 256, 128], P('blk', 'cell')
- triad_sums: float32 [2, 64, 64], replicated
Inputs may be any that keep to these rules, and one draw needn't show every extreme that they name: `block_list`: each row (K, L) holds two frequency block numbers with K + L <= 2; no row appears twice. counts[n] offsets 0 .. counts[n] - 1 of block L are live; some listed pair has all 64 offsets live in every draw.
All inputs are finite; a program needn't handle non-finite values.
Results may differ from a plain program's by a relative error of at most 0.0003.
Values may be sent and summed in bfloat16 or wider, within the bound.
A program may use at most 128 MiB of HBM per device.

v0:
```python
import math
import jax
import jax.numpy as jnp
from jax import lax
from jax.sharding import PartitionSpec as P

FBLK = 64
CZ = 16


def with_halo(cells, sides, width):
    for axis, dim in sides:
        count = lax.axis_size(axis)
        ends = count - 1
        head = lax.slice_in_dim(cells, 0, width, axis=dim)
        tail = lax.slice_in_dim(cells, cells.shape[dim] - width, cells.shape[dim], axis=dim)
        cells = jnp.concatenate(
            [
                lax.ppermute(tail, axis, [(i, (i + 1) % count) for i in range(ends)]),
                cells,
                lax.ppermute(head, axis, [((i + 1) % count, i) for i in range(ends)]),
            ],
            axis=dim,
        )
    return cells


def ahead(values, stride):
    filler = jnp.zeros(values.shape[:-1] + (stride,), values.dtype)
    return jnp.concatenate([values[..., stride:], filler], axis=-1)


def behind(values, stride):
    filler = jnp.zeros(values.shape[:-1] + (stride,), values.dtype)
    return jnp.concatenate([filler, values[..., :-stride]], axis=-1)


def group_density(donor_modes, slopes, receiver):
    accumulated = 0.0
    for component in range(3):
        real_sum = 0.0
        imag_sum = 0.0
        for direction in range(3):
            grad_real = slopes[direction][:, component, 0][:, :, None]
            grad_imag = slopes[direction][:, component, 1][:, :, None]
            donor_real = donor_modes[:, direction, 0][:, None]
            donor_imag = donor_modes[:, direction, 1][:, None]
            real_sum = real_sum + donor_real * grad_real - donor_imag * grad_imag
            imag_sum = imag_sum + donor_real * grad_imag + donor_imag * grad_real
        accumulated = (
            accumulated
            + receiver[:, component, 0] * real_sum
            + receiver[:, component, 1] * imag_sum
        )
    return -jnp.sum(accumulated, axis=0)


def per_device(velocity_modes, block_list, counts):
    blocks_here, _, _, freq_count, planes, cross_cells = velocity_modes.shape
    block_width = FBLK
    donors_span = (freq_count // block_width - 1) * block_width
    welch_all = blocks_here * lax.axis_size("blk")
    cells_all = planes * lax.axis_size("cell") * cross_cells
    scale_field = 0.25 / math.sqrt(welch_all * block_width)
    scale_triad = 0.25 / math.sqrt(welch_all * cells_all)
    extended = with_halo(velocity_modes, (("cell", 4),), 1)
    group_size = math.gcd(16, block_width)
    turn_count = block_width // group_size
    z_position = lax.broadcasted_iota(jnp.int32, (cross_cells,), 0) % CZ
    keep_upper = (z_position != CZ - 1).astype(jnp.float32)
    keep_lower = (z_position != 0).astype(jnp.float32)
    offsets_group = jnp.arange(group_size, dtype=jnp.int32)
    transfer = jnp.zeros((donors_span, planes, cross_cells), jnp.float32)
    totals_list = []
    for listed in range(block_list.shape[0]):
        start_k = block_list[listed, 0] * block_width
        start_l = block_list[listed, 1] * block_width
        live_count = counts[listed]
        donor_modes = lax.dynamic_slice_in_dim(velocity_modes, start_k, block_width, 3).astype(
            jnp.float32
        )

        def one_turn(running, turn_index):
            first_freq = start_l + turn_index * group_size
            extended_part = lax.dynamic_slice_in_dim(extended, first_freq, group_size, 3).astype(
                jnp.float32
            )
            inner_part = lax.dynamic_slice_in_dim(velocity_modes, first_freq, group_size, 3).astype(
                jnp.float32
            )
            window = lax.dynamic_slice_in_dim(
                velocity_modes, start_k + first_freq, block_width + group_size - 1, 3
            ).astype(jnp.float32)
            slope_first = (extended_part[..., 2:, :] - extended_part[..., :-2, :]) * 0.5
            slope_second = (ahead(inner_part, CZ) - behind(inner_part, CZ)) * 0.5
            slope_third = (
                ahead(inner_part, 1) * keep_upper - behind(inner_part, 1) * keep_lower
            ) * 0.5
            receiver = jnp.stack(
                [window[:, :, :, offset : offset + block_width] for offset in range(group_size)],
                axis=3,
            )
            density = group_density(donor_modes, (slope_first, slope_second, slope_third), receiver)
            live = turn_index * group_size + offsets_group < live_count
            density = jnp.where(live[:, None, None, None], density, 0.0)
            return (running + jnp.sum(density, axis=0), jnp.sum(density, axis=(2, 3)))

        summed, columns = lax.scan(
            one_turn,
            jnp.zeros((block_width, planes, cross_cells), jnp.float32),
            jnp.arange(turn_count, dtype=jnp.int32),
        )
        current = lax.dynamic_slice_in_dim(transfer, start_k, block_width, 0)
        transfer = lax.dynamic_update_slice_in_dim(transfer, current + summed, start_k, 0)
        totals_list.append(columns.reshape(block_width, block_width).T)
    triads_local = jnp.stack(totals_list) * scale_triad
    triad_sums = lax.psum(triads_local, ("cell", "blk"))
    local_field = transfer * scale_field
    whole_field = lax.psum(local_field, "blk")
    share_rows = donors_span // lax.axis_size("blk")
    field_share = lax.dynamic_slice_in_dim(
        whole_field, lax.axis_index("blk") * share_rows, share_rows, 0
    )
    return (field_share, triad_sums)


def solution(mesh):
    return jax.shard_map(
        per_device,
        mesh=mesh,
        in_specs=(P("blk", None, None, None, "cell", None), P(), P()),
        out_specs=(P("blk", "cell", None), P()),
        check_vma=False,
    )
```

profile of v0, /device:TPU:1, one launch (start us, length us, event | category | flops | bytes accessed | tf_op | source)
XLA Modules:
  0.0 577.8 jit_solution(4235348865583273882)
XLA Ops:
  7.2 5.1 fusion.81
  13.3 4.9 collective-permute-start
  19.3 2.3 collective-permute-start.1
  23.6 3.2 copy.268
  28.8 3.6 dynamic-slice_convert_fusion.6
  32.3 2.5 copy.265
  34.9 2.5 copy.267
  37.5 6.8 %pad_maximum_fusion = bf16[2,3,2,256,6,128]{5,4,3,0,2,1:T(8,128)(2,1)} fusion(bf16[2,3,2,256,1,128]{5,4,3,0,2,1:T(2,128)(2,1)S(1)} %copy.267, bf16[2,3,2,256,1,128]{5,4,3,0,2,1:T(2,128)(2,1)S(1)} %copy.265, bf16[2,3,2,256,4,128]{5,4,3,2,1,0:T(4,128)(2,1)S(1)} %copy-done.2), kind=kLoop, calls=%fused_computation.188 | loop fusion | flops 14155776 | bytes 9437184 | tf_op jit(solution)/shard_map/concatenate | solution.py:17
  44.9 220.3 %while.27 = (s32[]{:T(128)}, f32[64,4,128]{2,0,1:T(8,128)S(1)}, f32[4,16,64]{2,1,0:T(8,128)}, s32[4]{0:T(128)S(1)}, s32[]{:T(128)}, /*index=5*/s32[]{:T(128)}, s...) while((s32[]{:T(128)}, f32[64,4,128]{2,0,1:T(8,128)S(1)}, ...), condition=%wide.region_9.10_spmd.clone, body=%wide.region_5.9_spmd.clone.sunk | while | flops 84912424 | bytes 105542472 | solution.py:108
  69.6 26.0 %fusion.279 = f32[16,64,4,128]{3,2,1,0:T(4,128)S(1)} fusion(f32[2,3,2,16,64,4,128]{6,5,4,0,2,1,3:T(4,128)} %fusion.275, f32[2,64,4,128]{3,2,1,0:T(4,128)S(1)} %get-tuple-element.580, f32[2,64,4,128]{3,2,1,0:T(4,128)S(1)} %get-tuple-element.581, f32[2,64,4,128]{3,2,1,0:T(4,128)S(1)} %get-tuple-element.582, ...), kind=kLoop, calls=%fused_computation.100.clone.1 | loop fusion | flops 81264640 | bytes 30015488 | tf_op jit(solution)/shard_map/while/body/eval_jaxpr/reduce_sum | solution.py:55
  96.3 3.0 fusion.281
  107.7 1.4 fusion.265
  124.7 26.0 %fusion.279 = f32[16,64,4,128]{3,2,1,0:T(4,128)S(1)} fusion(f32[2,3,2,16,64,4,128]{6,5,4,0,2,1,3:T(4,128)} %fusion.275, f32[2,64,4,128]{3,2,1,0:T(4,128)S(1)} %get-tuple-element.580, f32[2,64,4,128]{3,2,1,0:T(4,128)S(1)} %get-tuple-element.581, f32[2,64,4,128]{3,2,1,0:T(4,128)S(1)} %get-tuple-element.582, ...), kind=kLoop, calls=%fused_computation.100.clone.1 | loop fusion | flops 81264640 | bytes 30015488 | tf_op jit(solution)/shard_map/while/body/eval_jaxpr/reduce_sum | solution.py:55
  151.3 3.0 fusion.281
  179.7 26.0 %fusion.279 = f32[16,64,4,128]{3,2,1,0:T(4,128)S(1)} fusion(f32[2,3,2,16,64,4,128]{6,5,4,0,2,1,3:T(4,128)} %fusion.275, f32[2,64,4,128]{3,2,1,0:T(4,128)S(1)} %get-tuple-element.580, f32[2,64,4,128]{3,2,1,0:T(4,128)S(1)} %get-tuple-element.581, f32[2,64,4,128]{3,2,1,0:T(4,128)S(1)} %get-tuple-element.582, ...), kind=kLoop, calls=%fused_computation.100.clone.1 | loop fusion | flops 81264640 | bytes 30015488 | tf_op jit(solution)/shard_map/while/body/eval_jaxpr/reduce_sum | solution.py:55
  206.4 3.0 fusion.281
  217.8 1.4 fusion.265
  234.8 26.0 %fusion.279 = f32[16,64,4,128]{3,2,1,0:T(4,128)S(1)} fusion(f32[2,3,2,16,64,4,128]{6,5,4,0,2,1,3:T(4,128)} %fusion.275, f32[2,64,4,128]{3,2,1,0:T(4,128)S(1)} %get-tuple-element.580, f32[2,64,4,128]{3,2,1,0:T(4,128)S(1)} %get-tuple-element.581, f32[2,64,4,128]{3,2,1,0:T(4,128)S(1)} %get-tuple-element.582, ...), kind=kLoop, calls=%fused_computation.100.clone.1 | loop fusion | flops 81264640 | bytes 30015488 | tf_op jit(solution)/shard_map/while/body/eval_jaxpr/reduce_sum | solution.py:55
  261.5 3.0 fusion.281
  265.8 221.3 %while.26 = (s32[]{:T(128)}, f32[64,4,128]{2,0,1:T(8,128)S(1)}, f32[4,16,64]{2,1,0:T(8,128)}, s32[4]{0:T(128)S(1)}, s32[]{:T(128)}, /*index=5*/s32[]{:T(128)}, s...) while((s32[]{:T(128)}, f32[64,4,128]{2,0,1:T(8,128)S(1)}, ...), condition=%wide.region_4.5_spmd.clone, body=%wide.region_0.4_spmd.clone.sunk | while | flops 84912424 | bytes 105542472 | solution.py:108
  273.7 1.4 fusion.225
  290.7 26.0 %fusion.239 = f32[16,64,4,128]{3,2,1,0:T(4,128)S(1)} fusion(f32[2,3,2,16,64,4,128]{6,5,4,0,2,1,3:T(4,128)} %fusion.235, f32[2,64,4,128]{3,2,1,0:T(4,128)S(1)} %get-tuple-element.538, f32[2,64,4,128]{3,2,1,0:T(4,128)S(1)} %get-tuple-element.539, f32[2,64,4,128]{3,2,1,0:T(4,128)S(1)} %get-tuple-element.540, ...), kind=kLoop, calls=%fused_computation.9.clone.1 | loop fusion | flops 81264640 | bytes 30015488 | tf_op jit(solution)/shard_map/while/body/eval_jaxpr/reduce_sum | solution.py:55
  317.4 3.0 fusion.241
  346.0 26.0 %fusion.239 = f32[16,64,4,128]{3,2,1,0:T(4,128)S(1)} fusion(f32[2,3,2,16,64,4,128]{6,5,4,0,2,1,3:T(4,128)} %fusion.235, f32[2,64,4,128]{3,2,1,0:T(4,128)S(1)} %get-tuple-element.538, f32[2,64,4,128]{3,2,1,0:T(4,128)S(1)} %get-tuple-element.539, f32[2,64,4,128]{3,2,1,0:T(4,128)S(1)} %get-tuple-element.540, ...), kind=kLoop, calls=%fused_computation.9.clone.1 | loop fusion | flops 81264640 | bytes 30015488 | tf_op jit(solution)/shard_map/while/body/eval_jaxpr/reduce_sum | solution.py:55
  372.8 3.0 fusion.241
  384.4 1.4 fusion.225
  401.4 26.0 %fusion.239 = f32[16,64,4,128]{3,2,1,0:T(4,128)S(1)} fusion(f32[2,3,2,16,64,4,128]{6,5,4,0,2,1,3:T(4,128)} %fusion.235, f32[2,64,4,128]{3,2,1,0:T(4,128)S(1)} %get-tuple-element.538, f32[2,64,4,128]{3,2,1,0:T(4,128)S(1)} %get-tuple-element.539, f32[2,64,4,128]{3,2,1,0:T(4,128)S(1)} %get-tuple-element.540, ...), kind=kLoop, calls=%fused_computation.9.clone.1 | loop fusion | flops 81264640 | bytes 30015488 | tf_op jit(solution)/shard_map/while/body/eval_jaxpr/reduce_sum | solution.py:55
  428.1 3.0 fusion.241
  456.7 26.0 %fusion.239 = f32[16,64,4,128]{3,2,1,0:T(4,128)S(1)} fusion(f32[2,3,2,16,64,4,128]{6,5,4,0,2,1,3:T(4,128)} %fusion.235, f32[2,64,4,128]{3,2,1,0:T(4,128)S(1)} %get-tuple-element.538, f32[2,64,4,128]{3,2,1,0:T(4,128)S(1)} %get-tuple-element.539, f32[2,64,4,128]{3,2,1,0:T(4,128)S(1)} %get-tuple-element.540, ...), kind=kLoop, calls=%fused_computation.9.clone.1 | loop fusion | flops 81264640 | bytes 30015488 | tf_op jit(solution)/shard_map/while/body/eval_jaxpr/reduce_sum | solution.py:55
  483.4 3.0 fusion.241
  489.1 79.7 %psum.15 = f32[2,64,64]{1,2,0:T(8,128)S(1)} all-reduce(f32[2,64,64]{1,2,0:T(8,128)S(1)} %maximum_multiply_fusion), channel_id=1, replica_groups=mesh['cell'=64,'blk'=4] {'cell','blk'}, use_global_device_ids=true, to_apply=%region_11.12 | all-reduce | flops 8192 | bytes 65536 | tf_op jit(solution)/shard_map/psum | solution.py:117
  569.5 1.5 constant_dynamic-slice_fusion
  (303 shorter events, 204.7 us)
Async XLA Ops:
  7.2 14.5 %copy-start.3 = (s32[2,2]{1,0:T(2,128)S(1)}, s32[2,2]{1,0:T(2,128)}, u32[]{:S(2)}) copy-start(s32[2,2]{1,0:T(2,128)} %param.8) | copy-start | bytes 52
  7.2 562.3 %all-reduce.10.cloned.1.call-start = ((), (), s32[]{:S(2)}) async-start(), calls=%async_computation | async-start | bytes 786432 | tf_op jit(solution)/shard_map/psum | solution.py:119
  13.3 19.0 %collective-permute-start = (bf16[2,3,2,256,1,128]{5,3,4,2,1,0:T(8,128)(2,1)}, bf16[2,3,2,256,1,128]{5,3,4,2,1,0:T(8,128)(2,1)}, u32[]{:S(2)}, u32[]{:S(2)}) collective-permute-start(bf16[2,3,2,256,1,128]{5,3,4,2,1,0:T(8,128)(2,1)} %copy.288), channel_id=1, source_target_pairs={{0,4},{4,8},{8,12},{12,16},{16,20},{20,24},{24,28},{28,32},{32,36}... | collective-permute-start | bytes 2359304 | tf_op jit(solution)/shard_map/ppermute | solution.py:19
  18.2 9.9 %copy-start.4 = (s32[2]{0:T(128)S(1)}, s32[2]{0:T(128)}, u32[]{:S(2)}) copy-start(s32[2]{0:T(128)} %param.9) | copy-start | bytes 28
  19.3 15.6 %collective-permute-start.1 = (bf16[2,3,2,256,1,128]{5,3,4,2,1,0:T(8,128)(2,1)}, bf16[2,3,2,256,1,128]{5,3,4,2,1,0:T(8,128)(2,1)}, u32[]{:S(2)}, u32[]{:S(2)}) collective-permute-start(bf16[2,3,2,256,1,128]{5,3,4,2,1,0:T(8,128)(2,1)} %copy.289), channel_id=1, source_target_pairs={{4,0},{8,4},{12,8},{16,12},{20,16},{24,20},{28,24},{32,28},{36,32}... | collective-permute-start | bytes 2359304 | tf_op jit(solution)/shard_map/ppermute | solution.py:21
  28.8 8.7 %copy-start.2 = (bf16[2,3,2,256,4,128]{5,4,3,2,1,0:T(4,128)(2,1)S(1)}, bf16[2,3,2,256,4,128]{5,4,3,2,1,0:T(4,128)(2,1)}, u32[]{:S(2)}) copy-start(bf16[2,3,2,256,4,128]{5,4,3,2,1,0:T(4,128)(2,1)} %param.7) | copy-start | bytes 9437188
  67.3 2.2 copy-start.1
  122.4 2.2 copy-start.1
  177.4 2.2 copy-start.1
  232.5 2.2 copy-start.1
  288.4 2.2 copy-start
  343.7 2.2 copy-start
  399.1 2.2 copy-start
  454.4 2.2 copy-start
Sparse Core Ops, SparseCore 0:
  488.4 48.5 all-reduce.9
where the time goes:
time: 579 us; the launch traced here: 578 us
  other arithmetic  266 us (46%)
  local copies, waits for them, and re-layouts  202 us (35%)
  blocking collectives  79.7 us (14%)
  between operations  16.8 us (3%)
  starting transfers between devices  7.28 us (1%)
  loops' own time  6.1 us (1%)
    reduce_sum x8, other arithmetic, group_density(): return -jnp.sum(accumulated, axis=0)  208 us
    while x136, local copies, waits for them, and re-layouts  156 us
    psum x1, blocking collectives, per_device(): triad_sums = lax.psum(triads_local, ('cell', 'blk'))  79.7 us
    reduce_sum x8, other arithmetic, one_turn(): return (running + jnp.sum(density, axis=0), jnp.sum(density, axis=(2, 3)))  24.4 us
  transfers between devices with their start and end apart: 3, of which 0 were waited for; matrix products, arithmetic and copies ran while one was open for 2% of the time, Pallas kernels for 0%

commit v1 on v0

--- a/solution.py
+++ b/solution.py
@@ -114,7 +114,8 @@
         transfer = lax.dynamic_update_slice_in_dim(transfer, current + summed, start_k, 0)
         totals_list.append(columns.reshape(block_width, block_width).T)
     triads_local = jnp.stack(totals_list) * scale_triad
-    triad_sums = lax.psum(triads_local, ("cell", "blk"))
+    half = lax.psum(triads_local, "cell")
+    triad_sums = lax.psum(half, "blk")
     local_field = transfer * scale_field
     whole_field = lax.psum(local_field, "blk")
     share_rows = donors_span // lax.axis_size("blk")

time: 579 us -> 766 us (1.32)
  blocking collectives: 79.7 us -> 262 us
    psum x1 -> x2, blocking collectives: 79.7 us -> 262 us  [the longest x1 248 us: per_device(): half = lax.psum(triads_local, 'cell')]
where the time goes in v1:
time: 766 us; the launch traced here: 759 us
  other arithmetic  265 us (35%)
  blocking collectives  262 us (34%)
  local copies, waits for them, and re-layouts  202 us (26%)
  between operations  16.7 us (2%)
    psum x1, blocking collectives, per_device(): half = lax.psum(triads_local, 'cell')  248 us
    reduce_sum x8, other arithmetic, group_density(): return -jnp.sum(accumulated, axis=0)  208 us
    while x136, local copies, waits for them, and re-layouts  156 us
    reduce_sum x8, other arithmetic, one_turn(): return (running + jnp.sum(density, axis=0), jnp.sum(density, axis=(2, 3)))  24.4 us
  transfers between devices with their start and end apart: 3, of which 0 were waited for; matrix products, arithmetic and copies ran while one was open for 2% of the time, Pallas kernels for 0%

profile of v1, /device:TPU:1, one launch (start us, length us, event | category | flops | bytes accessed | tf_op | source)
XLA Modules:
  0.0 759.1 jit_solution(600797913929713117)
XLA Ops:
  7.2 5.1 fusion.81
  13.3 4.9 collective-permute-start
  19.3 2.3 collective-permute-start.1
  23.6 3.2 copy.268
  28.6 3.6 dynamic-slice_convert_fusion.6
  32.2 2.5 copy.265
  34.8 2.5 copy.267
  37.3 6.8 pad_maximum_fusion
  44.8 220.9 %while.27 = (s32[]{:T(128)}, f32[64,4,128]{2,0,1:T(8,128)S(1)}, f32[4,16,64]{2,1,0:T(8,128)}, s32[4]{0:T(128)S(1)}, s32[]{:T(128)}, /*index=5*/s32[]{:T(128)}, s...) while((s32[]{:T(128)}, f32[64,4,128]{2,0,1:T(8,128)S(1)}, ...), condition=%wide.region_9.10_spmd.clone, body=%wide.region_5.9_spmd.clone.sunk | while | flops 84912424 | bytes 105542472 | solution.py:108
  52.6 1.4 fusion.265
  69.6 26.0 %fusion.279 = f32[16,64,4,128]{3,2,1,0:T(4,128)S(1)} fusion(f32[2,3,2,16,64,4,128]{6,5,4,0,2,1,3:T(4,128)} %fusion.275, f32[2,64,4,128]{3,2,1,0:T(4,128)S(1)} %get-tuple-element.580, f32[2,64,4,128]{3,2,1,0:T(4,128)S(1)} %get-tuple-element.581, f32[2,64,4,128]{3,2,1,0:T(4,128)S(1)} %get-tuple-element.582, ...), kind=kLoop, calls=%fused_computation.100.clone.1 | loop fusion | flops 81264640 | bytes 30015488 | tf_op jit(solution)/shard_map/while/body/eval_jaxpr/reduce_sum | solution.py:55
  96.3 3.0 fusion.281
  107.9 1.4 fusion.265
  124.8 26.0 %fusion.279 = f32[16,64,4,128]{3,2,1,0:T(4,128)S(1)} fusion(f32[2,3,2,16,64,4,128]{6,5,4,0,2,1,3:T(4,128)} %fusion.275, f32[2,64,4,128]{3,2,1,0:T(4,128)S(1)} %get-tuple-element.580, f32[2,64,4,128]{3,2,1,0:T(4,128)S(1)} %get-tuple-element.581, f32[2,64,4,128]{3,2,1,0:T(4,128)S(1)} %get-tuple-element.582, ...), kind=kLoop, calls=%fused_computation.100.clone.1 | loop fusion | flops 81264640 | bytes 30015488 | tf_op jit(solution)/shard_map/while/body/eval_jaxpr/reduce_sum | solution.py:55
  151.5 3.0 fusion.281
  163.1 1.4 fusion.265
  180.1 26.0 %fusion.279 = f32[16,64,4,128]{3,2,1,0:T(4,128)S(1)} fusion(f32[2,3,2,16,64,4,128]{6,5,4,0,2,1,3:T(4,128)} %fusion.275, f32[2,64,4,128]{3,2,1,0:T(4,128)S(1)} %get-tuple-element.580, f32[2,64,4,128]{3,2,1,0:T(4,128)S(1)} %get-tuple-element.581, f32[2,64,4,128]{3,2,1,0:T(4,128)S(1)} %get-tuple-element.582, ...), kind=kLoop, calls=%fused_computation.100.clone.1 | loop fusion | flops 81264640 | bytes 30015488 | tf_op jit(solution)/shard_map/while/body/eval_jaxpr/reduce_sum | solution.py:55
  206.7 3.0 fusion.281
  235.3 26.0 %fusion.279 = f32[16,64,4,128]{3,2,1,0:T(4,128)S(1)} fusion(f32[2,3,2,16,64,4,128]{6,5,4,0,2,1,3:T(4,128)} %fusion.275, f32[2,64,4,128]{3,2,1,0:T(4,128)S(1)} %get-tuple-element.580, f32[2,64,4,128]{3,2,1,0:T(4,128)S(1)} %get-tuple-element.581, f32[2,64,4,128]{3,2,1,0:T(4,128)S(1)} %get-tuple-element.582, ...), kind=kLoop, calls=%fused_computation.100.clone.1 | loop fusion | flops 81264640 | bytes 30015488 | tf_op jit(solution)/shard_map/while/body/eval_jaxpr/reduce_sum | solution.py:55
  262.0 3.0 fusion.281
  266.3 220.2 %while.26 = (s32[]{:T(128)}, f32[64,4,128]{2,0,1:T(8,128)S(1)}, f32[4,16,64]{2,1,0:T(8,128)}, s32[4]{0:T(128)S(1)}, s32[]{:T(128)}, /*index=5*/s32[]{:T(128)}, s...) while((s32[]{:T(128)}, f32[64,4,128]{2,0,1:T(8,128)S(1)}, ...), condition=%wide.region_4.5_spmd.clone, body=%wide.region_0.4_spmd.clone.sunk | while | flops 84912424 | bytes 105542472 | solution.py:108
  291.0 26.0 %fusion.239 = f32[16,64,4,128]{3,2,1,0:T(4,128)S(1)} fusion(f32[2,3,2,16,64,4,128]{6,5,4,0,2,1,3:T(4,128)} %fusion.235, f32[2,64,4,128]{3,2,1,0:T(4,128)S(1)} %get-tuple-element.538, f32[2,64,4,128]{3,2,1,0:T(4,128)S(1)} %get-tuple-element.539, f32[2,64,4,128]{3,2,1,0:T(4,128)S(1)} %get-tuple-element.540, ...), kind=kLoop, calls=%fused_computation.9.clone.1 | loop fusion | flops 81264640 | bytes 30015488 | tf_op jit(solution)/shard_map/while/body/eval_jaxpr/reduce_sum | solution.py:55
  317.6 3.0 fusion.241
  346.1 26.0 %fusion.239 = f32[16,64,4,128]{3,2,1,0:T(4,128)S(1)} fusion(f32[2,3,2,16,64,4,128]{6,5,4,0,2,1,3:T(4,128)} %fusion.235, f32[2,64,4,128]{3,2,1,0:T(4,128)S(1)} %get-tuple-element.538, f32[2,64,4,128]{3,2,1,0:T(4,128)S(1)} %get-tuple-element.539, f32[2,64,4,128]{3,2,1,0:T(4,128)S(1)} %get-tuple-element.540, ...), kind=kLoop, calls=%fused_computation.9.clone.1 | loop fusion | flops 81264640 | bytes 30015488 | tf_op jit(solution)/shard_map/while/body/eval_jaxpr/reduce_sum | solution.py:55
  372.7 3.0 fusion.241
  401.1 26.0 %fusion.239 = f32[16,64,4,128]{3,2,1,0:T(4,128)S(1)} fusion(f32[2,3,2,16,64,4,128]{6,5,4,0,2,1,3:T(4,128)} %fusion.235, f32[2,64,4,128]{3,2,1,0:T(4,128)S(1)} %get-tuple-element.538, f32[2,64,4,128]{3,2,1,0:T(4,128)S(1)} %get-tuple-element.539, f32[2,64,4,128]{3,2,1,0:T(4,128)S(1)} %get-tuple-element.540, ...), kind=kLoop, calls=%fused_computation.9.clone.1 | loop fusion | flops 81264640 | bytes 30015488 | tf_op jit(solution)/shard_map/while/body/eval_jaxpr/reduce_sum | solution.py:55
  427.7 3.0 fusion.241
  456.2 26.0 %fusion.239 = f32[16,64,4,128]{3,2,1,0:T(4,128)S(1)} fusion(f32[2,3,2,16,64,4,128]{6,5,4,0,2,1,3:T(4,128)} %fusion.235, f32[2,64,4,128]{3,2,1,0:T(4,128)S(1)} %get-tuple-element.538, f32[2,64,4,128]{3,2,1,0:T(4,128)S(1)} %get-tuple-element.539, f32[2,64,4,128]{3,2,1,0:T(4,128)S(1)} %get-tuple-element.540, ...), kind=kLoop, calls=%fused_computation.9.clone.1 | loop fusion | flops 81264640 | bytes 30015488 | tf_op jit(solution)/shard_map/while/body/eval_jaxpr/reduce_sum | solution.py:55
  482.8 3.0 fusion.241
  488.5 247.5 %psum.22 = f32[2,64,64]{1,2,0:T(8,128)S(1)} all-reduce(f32[2,64,64]{1,2,0:T(8,128)S(1)} %maximum_multiply_fusion), channel_id=1, replica_groups=mesh['cell'=64,'blk'=4] {'cell'}, use_global_device_ids=true, to_apply=%region_11.12 | all-reduce | flops 8192 | bytes 65536 | tf_op jit(solution)/shard_map/psum | solution.py:117
  736.0 14.0 %psum.23 = f32[2,64,64]{1,2,0:T(8,128)S(1)} all-reduce(f32[2,64,64]{1,2,0:T(8,128)S(1)} %psum.22), channel_id=1, replica_groups=mesh['cell'=64,'blk'=4] {'blk'}, use_global_device_ids=true, to_apply=%region_12.13 | all-reduce | flops 8192 | bytes 65536 | tf_op jit(solution)/shard_map/psum | solution.py:118
  750.7 1.5 constant_dynamic-slice_fusion
  (304 shorter events, 205.7 us)
Async XLA Ops:
  7.2 14.5 %copy-start.3 = (s32[2,2]{1,0:T(2,128)S(1)}, s32[2,2]{1,0:T(2,128)}, u32[]{:S(2)}) copy-start(s32[2,2]{1,0:T(2,128)} %param.8) | copy-start | bytes 52
  7.2 743.6 %all-reduce.10.cloned.1.call-start = ((), (), s32[]{:S(2)}) async-start(), calls=%async_computation | async-start | bytes 786432 | tf_op jit(solution)/shard_map/psum | solution.py:120
  13.3 18.9 %collective-permute-start = (bf16[2,3,2,256,1,128]{5,3,4,2,1,0:T(8,128)(2,1)}, bf16[2,3,2,256,1,128]{5,3,4,2,1,0:T(8,128)(2,1)}, u32[]{:S(2)}, u32[]{:S(2)}) collective-permute-start(bf16[2,3,2,256,1,128]{5,3,4,2,1,0:T(8,128)(2,1)} %copy.288), channel_id=1, source_target_pairs={{0,4},{4,8},{8,12},{12,16},{16,20},{20,24},{24,28},{28,32},{32,36}... | collective-permute-start | bytes 2359304 | tf_op jit(solution)/shard_map/ppermute | solution.py:19
  18.3 9.8 %copy-start.4 = (s32[2]{0:T(128)S(1)}, s32[2]{0:T(128)}, u32[]{:S(2)}) copy-start(s32[2]{0:T(128)} %param.9) | copy-start | bytes 28
  19.3 15.4 %collective-permute-start.1 = (bf16[2,3,2,256,1,128]{5,3,4,2,1,0:T(8,128)(2,1)}, bf16[2,3,2,256,1,128]{5,3,4,2,1,0:T(8,128)(2,1)}, u32[]{:S(2)}, u32[]{:S(2)}) collective-permute-start(bf16[2,3,2,256,1,128]{5,3,4,2,1,0:T(8,128)(2,1)} %copy.289), channel_id=1, source_target_pairs={{4,0},{8,4},{12,8},{16,12},{20,16},{24,20},{28,24},{32,28},{36,32}... | collective-permute-start | bytes 2359304 | tf_op jit(solution)/shard_map/ppermute | solution.py:21
  28.6 8.7 %copy-start.2 = (bf16[2,3,2,256,4,128]{5,4,3,2,1,0:T(4,128)(2,1)S(1)}, bf16[2,3,2,256,4,128]{5,4,3,2,1,0:T(4,128)(2,1)}, u32[]{:S(2)}) copy-start(bf16[2,3,2,256,4,128]{5,4,3,2,1,0:T(4,128)(2,1)} %param.7) | copy-start | bytes 9437188
  67.3 2.2 copy-start.1
  122.6 2.2 copy-start.1
  177.8 2.2 copy-start.1
  233.0 2.2 copy-start.1
  288.7 2.2 copy-start
  343.8 2.2 copy-start
  398.8 2.2 copy-start
  453.9 2.2 copy-start
Sparse Core Ops, SparseCore 0:
  487.8 48.7 all-reduce.9
